TPU v7x, 256 devices: a whole 4x4x8 slice. The times are simulated.
256 devices in a mesh: pipe: 8 (over z), dp: 4 (over y), expert: 8 (over x, core).
Axes of the slice: x: 4, y: 4, z: 8, core: 2. Of those that a mesh axis runs over, the one named last changes fastest.
Arguments:
- tokens: bfloat16 [4096, 4096], P(('dp', 'expert'), 'pipe'), may hold values from -6 to 6
- routes: int32 [4096, 6], P(('dp', 'expert')), may hold values from 0 to 31, all different within a row; in each aligned block of 128 rows (0 to 127, 128 to 255, ...) at most 32 rows name the same one
- gates: float32 [4096, 6], P(('dp', 'expert')), may hold values from 0.1 to 0.5
- w_gate: bfloat16 [32, 4096, 1024], P(('dp', 'expert'), 'pipe'), may hold values from -0.09375 to 0.09375
- w_up: bfloat16 [32, 4096, 1024], P(('dp', 'expert'), 'pipe'), may hold values from -0.09375 to 0.09375
- w_down: bfloat16 [32, 1024, 4096], P(('dp', 'expert'), None, 'pipe'), may hold values from -0.1875 to 0.1875
- grad_out: bfloat16 [4096, 4096], P(('dp', 'expert'), 'pipe'), may hold values from -6 to 6
Outputs:
- mixed: bfloat16 [4096, 4096], P(('dp', 'expert'), 'pipe')
- grad_tokens: bfloat16 [4096, 4096], P(('dp', 'expert'), 'pipe')
- grad_gate: bfloat16 [32, 4096, 1024], P(('dp', 'expert'), 'pipe')
- grad_up: bfloat16 [32, 4096, 1024], P(('dp', 'expert'), 'pipe')
- grad_down: bfloat16 [32, 1024, 4096], P(('dp', 'expert'), None, 'pipe')
Inputs may be any that keep to these rules, and one draw needn't show every extreme that they name: `routes`: each row names 6 different experts; in each aligned block of 128 rows no expert is named by more than 32 rows, a bound that some block reaches.
All inputs are finite; a program needn't handle non-finite values.
Results may differ from a plain program's by a relative error of at most 0.0065.
Values may be sent and summed in bfloat16 or wider, within the bound.
A program may use at most 128 MiB of HBM per device.

v0:
```python
import jax
import jax.numpy as jnp
from jax import lax
from jax.sharding import PartitionSpec as P

CAP = 32


def slot_layout(routes, num_experts):
    tok_count, top_count = routes.shape
    chosen = routes.reshape(tok_count * top_count)
    expert_ids = jnp.arange(num_experts, dtype=jnp.int32)
    onehot = (chosen[:, None] == expert_ids[None, :]).astype(jnp.int32)
    earlier = jnp.cumsum(onehot, axis=0) - onehot
    position = jnp.sum(earlier * onehot, axis=1)
    target = chosen * CAP + position
    slot_ids = jnp.arange(num_experts * CAP, dtype=jnp.int32)
    placed = slot_ids[:, None] == target[None, :]
    return placed.reshape(num_experts * CAP, tok_count, top_count)


def local(tokens, routes, gates, w_gate, w_up, w_down, grad_out):
    groups = lax.axis_size(("dp", "expert"))
    local_experts = w_gate.shape[0]
    num_experts = local_experts * groups
    slice_width = tokens.shape[1]
    placed = slot_layout(routes, num_experts)
    dispatch = jnp.sum(placed.astype(jnp.int32), axis=2).astype(jnp.bfloat16)
    mixing = jnp.sum(jnp.where(placed, gates[None, :, :], 0.0), axis=2)
    outbound = jnp.dot(dispatch, tokens, preferred_element_type=jnp.float32).astype(jnp.bfloat16)
    outbound = outbound.reshape(num_experts, CAP, slice_width)
    scaled_out = jnp.dot(
        mixing, grad_out.astype(jnp.float32), precision=lax.Precision.HIGHEST
    ).astype(jnp.bfloat16)
    scaled_out = scaled_out.reshape(num_experts, CAP, slice_width)
    arrived, arrived_grad = (
        lax.all_to_all(outbound, ("dp", "expert"), split_axis=0, concat_axis=0, tiled=True),
        lax.all_to_all(scaled_out, ("dp", "expert"), split_axis=0, concat_axis=0, tiled=True),
    )
    expert_rows = arrived.reshape(groups, local_experts, CAP, slice_width)
    scaled = arrived_grad.reshape(groups, local_experts, CAP, slice_width)
    gate_part = jnp.einsum(
        "sjcd,jdf->sjcf", expert_rows, w_gate, preferred_element_type=jnp.float32
    )
    up_part = jnp.einsum("sjcd,jdf->sjcf", expert_rows, w_up, preferred_element_type=jnp.float32)
    gate_share, up_share = (
        lax.psum_scatter(gate_part, "pipe", scatter_dimension=3, tiled=True),
        lax.psum_scatter(up_part, "pipe", scatter_dimension=3, tiled=True),
    )
    hidden_share = (jax.nn.silu(gate_share) * up_share).astype(jnp.bfloat16)
    hidden = lax.all_gather(hidden_share, "pipe", axis=3, tiled=True)
    expert_out = jnp.einsum(
        "sjcf,jfd->sjcd", hidden, w_down, preferred_element_type=jnp.float32
    ).astype(jnp.bfloat16)
    returned = lax.all_to_all(
        expert_out.reshape(num_experts, CAP, slice_width),
        ("dp", "expert"),
        split_axis=0,
        concat_axis=0,
        tiled=True,
    )
    returned_rows = returned.reshape(num_experts * CAP, slice_width).astype(jnp.float32)
    mixed = jnp.dot(mixing.T, returned_rows, precision=lax.Precision.HIGHEST).astype(jnp.bfloat16)
    d_hidden_part = jnp.einsum("sjcd,jfd->sjcf", scaled, w_down, preferred_element_type=jnp.float32)
    d_hidden = lax.psum_scatter(d_hidden_part, "pipe", scatter_dimension=3, tiled=True)
    sig_gate = jax.nn.sigmoid(gate_share)
    d_gate_share = (d_hidden * up_share * sig_gate * (1.0 + gate_share * (1.0 - sig_gate))).astype(
        jnp.bfloat16
    )
    d_up_share = (d_hidden * gate_share * sig_gate).astype(jnp.bfloat16)
    d_gate, d_up = (
        lax.all_gather(d_gate_share, "pipe", axis=3, tiled=True),
        lax.all_gather(d_up_share, "pipe", axis=3, tiled=True),
    )
    d_rows = (
        jnp.einsum("sjcf,jdf->sjcd", d_gate, w_gate, preferred_element_type=jnp.float32)
        + jnp.einsum("sjcf,jdf->sjcd", d_up, w_up, preferred_element_type=jnp.float32)
    ).astype(jnp.bfloat16)
    back_rows = lax.all_to_all(
        d_rows.reshape(num_experts, CAP, slice_width),
        ("dp", "expert"),
        split_axis=0,
        concat_axis=0,
        tiled=True,
    )
    grad_tokens = jnp.dot(
        dispatch.T,
        back_rows.reshape(num_experts * CAP, slice_width),
        preferred_element_type=jnp.float32,
    ).astype(jnp.bfloat16)
    grad_gate = jnp.einsum(
        "sjcd,sjcf->jdf", expert_rows, d_gate, preferred_element_type=jnp.float32
    ).astype(jnp.bfloat16)
    grad_up = jnp.einsum(
        "sjcd,sjcf->jdf", expert_rows, d_up, preferred_element_type=jnp.float32
    ).astype(jnp.bfloat16)
    grad_down = jnp.einsum(
        "sjcf,sjcd->jfd", hidden, scaled, preferred_element_type=jnp.float32
    ).astype(jnp.bfloat16)
    return (mixed, grad_tokens, grad_gate, grad_up, grad_down)


def solution(mesh):
    placed = (
        P(("dp", "expert"), "pipe"),
        P(("dp", "expert"), None),
        P(("dp", "expert"), None),
        P(("dp", "expert"), "pipe", None),
        P(("dp", "expert"), "pipe", None),
        P(("dp", "expert"), None, "pipe"),
        P(("dp", "expert"), "pipe"),
    )
    return jax.shard_map(
        local,
        mesh=mesh,
        in_specs=placed,
        out_specs=(
            P(("dp", "expert"), "pipe"),
            P(("dp", "expert"), "pipe"),
            P(("dp", "expert"), "pipe", None),
            P(("dp", "expert"), "pipe", None),
            P(("dp", "expert"), None, "pipe"),
        ),
        check_vma=False,
    )
```

profile of v0, /device:TPU:1, one launch (start us, length us, event | category | flops | bytes accessed | tf_op | source)
XLA Modules:
  0.0 395.4 jit_solution(5158708211324095132)
XLA Ops:
  7.2 0.0 copy-start
  7.2 0.0 reduce-scatter.6.cloned.1.call-start
  7.2 0.9 copy.38
  8.1 0.1 eq.44
  8.2 0.1 eq.40
  8.4 1.7 reduce-window.6
  10.1 0.3 slice_reduce_fusion
  10.4 0.1 fusion.42
  10.5 0.1 reduce_sum.30
  10.7 0.1 copy.41
  10.7 0.7 multiply_add_fusion
  11.5 0.4 convert_reduce_fusion
  11.8 1.3 convolution_convert_fusion
  13.2 25.4 %all_to_all.20 = bf16[32,32,512]{2,1,0:T(8,128)(2,1)S(1)} all-to-all(bf16[32,32,512]{2,1,0:T(8,128)(2,1)S(1)} %bitcast.121), channel_id=1, replica_groups=mesh['pipe'=8,'dp'=4,'expert'=8] {'dp','expert'}, dimensions={0} | all-to-all | bytes 2097152 | tf_op jit(solution)/shard_map/all_to_all | solution.py:37
  38.6 0.0 copy-done.4
  38.6 3.2 convolution_bitcast_fusion.1
  41.8 0.0 reduce-scatter.6.cloned.1.call-update
  41.8 0.0 reduce-scatter.4.cloned.1.call-start
  41.9 4.4 %convolution_bitcast_fusion.2 = f32[32,1,32,1024]{3,2,0,1:T(8,128)} fusion(bf16[32,32,512]{2,1,0:T(8,128)(2,1)S(1)} %all_to_all.20, bf16[1,512,1024]{2,1,0:T(8,128)(2,1)} %param.10), kind=kOutput, calls=%fused_computation.5 | convolution fusion | flops 1073741824 | bytes 6291456 | tf_op jit(solution)/shard_map/sjcd,jdf->sjcf/dot_general | solution.py:42
  46.3 0.0 copy-start.6
  46.3 0.0 copy-start.5
  46.3 0.0 reduce-scatter.4.cloned.1.call-update
  46.4 0.0 reduce-scatter.8.cloned.1.call-start
  46.4 0.6 copy-done.6
  47.0 0.4 select_reduce_fusion
  47.4 0.0 copy-done.5
  47.4 1.0 convolution_convert_fusion.1
  48.4 20.7 %all_to_all.21 = bf16[32,32,512]{2,1,0:T(8,128)(2,1)S(1)} all-to-all(bf16[32,32,512]{2,1,0:T(8,128)(2,1)S(1)} %bitcast.122), channel_id=1, replica_groups=mesh['pipe'=8,'dp'=4,'expert'=8] {'dp','expert'}, dimensions={0} | all-to-all | bytes 2097152 | tf_op jit(solution)/shard_map/all_to_all | solution.py:38
  69.1 0.0 copy-start.1
  69.1 1.0 copy-done.1
  70.0 0.0 copy-done
  70.0 3.2 convolution_bitcast_fusion
  73.3 0.0 reduce-scatter.8.cloned.1.call-update
  73.3 0.0 all-gather.4.cloned.1.call-start
  73.3 23.0 %reduce-scatter.6.cloned.1.call-done = f32[32,1,32,128]{3,2,0,1:T(8,128)} async-done(((f32[32,1,32,1024]{3,2,0,1:T(8,128)}), f32[32,1,32,128]{3,2,0,1:T(8,128)}) %reduce-scatter.6.cloned.1.call-update) | async-done | bytes 524304 | tf_op jit(solution)/shard_map/reduce_scatter | solution.py:48
  96.3 56.5 %reduce-scatter.4.cloned.1.call-done = f32[32,1,32,128]{3,2,0,1:T(8,128)} async-done(((f32[32,1,32,1024]{3,2,0,1:T(8,128)}), f32[32,1,32,128]{3,2,0,1:T(8,128)}) %reduce-scatter.4.cloned.1.call-update) | async-done | bytes 524304 | tf_op jit(solution)/shard_map/reduce_scatter | solution.py:47
  152.9 56.6 %reduce-scatter.8.cloned.1.call-done = f32[32,1,32,128]{3,2,0,1:T(8,128)} async-done(((f32[32,1,32,1024]{3,2,0,1:T(8,128)}), f32[32,1,32,128]{3,2,0,1:T(8,128)}) %reduce-scatter.8.cloned.1.call-update) | async-done | bytes 524304 | tf_op jit(solution)/shard_map/reduce_scatter | solution.py:65
  209.4 2.5 multiply_convert_fusion.1
  211.9 0.0 all-gather.4.cloned.1.call-update
  212.0 0.0 all-gather.8.cloned.1.call-start
  212.0 0.5 all-gather.8.cloned.1.call-update
  212.6 0.0 all-gather.6.cloned.1.call-start
  212.6 0.5 all-gather.6.cloned.1.call-update
  213.1 40.6 %all-gather.4.cloned.1.call-done = bf16[32,1,32,1024]{3,2,0,1:T(8,128)(2,1)} async-done(((bf16[32,1,32,128]{3,2,0,1:T(8,128)(2,1)}), bf16[32,1,32,1024]{3,2,0,1:T(8,128)(2,1)}) %all-gather.4.cloned.1.call-update) | async-done | bytes 2097168 | tf_op jit(solution)/shard_map/all_gather | solution.py:51
  253.7 3.8 fusion.20
  257.6 12.2 %all-to-all-start.1 = ((bf16[32,32,512]{2,1,0:T(8,128)(2,1)}), bf16[32,32,512]{2,1,0:T(8,128)(2,1)}, u32[]{:S(2)}, u32[]{:S(2)}) async-start(bf16[32,32,512]{2,1,0:T(8,128)(2,1)} %fusion.20), calls=%async_computation.3 | async-start | bytes 2097152 | tf_op jit(solution)/shard_map/all_to_all | solution.py:55
  269.8 31.9 %all-gather.8.cloned.1.call-done = bf16[32,1,32,1024]{3,2,0,1:T(8,128)(2,1)} async-done(((bf16[32,1,32,128]{3,2,0,1:T(8,128)(2,1)}), bf16[32,1,32,1024]{3,2,0,1:T(8,128)(2,1)}) %all-gather.8.cloned.1.call-update) | async-done | bytes 2097168 | tf_op jit(solution)/shard_map/all_gather | solution.py:73
  301.7 0.0 copy-start.2
  301.7 0.0 copy-start.7
  301.7 4.6 %fusion.2 = f32[32,32,512]{2,1,0:T(8,128)} fusion(bf16[32,1,32,1024]{3,2,0,1:T(8,128)(2,1)} %all-gather.8.cloned.1.call-done, bf16[1,512,1024]{2,1,0:T(8,128)(2,1)} %param.11), kind=kOutput, calls=%fused_computation.11 | convolution fusion | flops 1073741824 | bytes 5242880 | tf_op jit(solution)/shard_map/sjcf,jdf->sjcd/dot_general | solution.py:77
  306.3 0.0 copy-done.2
  306.3 0.0 copy-done.7
  306.3 2.3 fusion.29
  308.6 41.2 %all-gather.6.cloned.1.call-done = bf16[32,1,32,1024]{3,2,0,1:T(8,128)(2,1)} async-done(((bf16[32,1,32,128]{3,2,0,1:T(8,128)(2,1)}), bf16[32,1,32,1024]{3,2,0,1:T(8,128)(2,1)}) %all-gather.6.cloned.1.call-update) | async-done | bytes 2097168 | tf_op jit(solution)/shard_map/all_gather | solution.py:72
  349.8 0.0 copy-start.3
  349.8 5.0 %add_convert_fusion = bf16[32,32,512]{2,1,0:T(8,128)(2,1)} fusion(f32[32,32,512]{2,1,0:T(8,128)} %fusion.2, bf16[32,1,32,1024]{3,2,0,1:T(8,128)(2,1)} %all-gather.6.cloned.1.call-done, bf16[1,512,1024]{2,1,0:T(8,128)(2,1)} %param.10), kind=kOutput, calls=%fused_computation.21 | convolution fusion | flops 1074790400 | bytes 6291456 | tf_op jit(solution)/shard_map/sjcf,jdf->sjcd/dot_general | solution.py:76
  354.8 0.0 copy-done.3
  354.8 2.2 fusion.26
  357.0 0.0 all-to-all-done.1
  357.0 12.2 %all-to-all-start.3 = ((bf16[32,32,512]{2,1,0:T(8,128)(2,1)}), bf16[32,32,512]{2,1,0:T(8,128)(2,1)}, u32[]{:S(2)}, u32[]{:S(2)}) async-start(bf16[32,32,512]{2,1,0:T(8,128)(2,1)} %add_convert_fusion), calls=%async_computation.6 | async-start | bytes 2097152 | tf_op jit(solution)/shard_map/all_to_all | solution.py:79
  369.2 3.8 fusion.23
  373.1 2.6 convolution_convert_fusion.3
  375.6 10.7 %all-to-all-done.3 = bf16[32,32,512]{2,1,0:T(8,128)(2,1)} async-done(((bf16[32,32,512]{2,1,0:T(8,128)(2,1)}), bf16[32,32,512]{2,1,0:T(8,128)(2,1)}, u32[]{:S(2)}, u32[]{:S(2)}) %all-to-all-start.3) | async-done | bytes 1048608 | tf_op jit(solution)/shard_map/all_to_all | solution.py:79
  386.3 2.2 convolution_convert_fusion.2
  (3 shorter events, 0.0 us)
Async XLA Ops:
  7.2 62.9 %copy-start = (bf16[1,1024,512]{2,1,0:T(8,128)(2,1)S(1)}, bf16[1,1024,512]{2,1,0:T(8,128)(2,1)}, u32[]{:S(2)}) copy-start(bf16[1,1024,512]{2,1,0:T(8,128)(2,1)} %param.12) | copy-start | bytes 3145732
  7.2 89.1 %reduce-scatter.6.cloned.1.call-start = ((), (), s32[]{:S(2)}) async-start(), calls=%async_computation.8 | async-start | bytes 4718592 | tf_op jit(solution)/shard_map/reduce_scatter | solution.py:48
  11.5 27.1 %copy-start.4 = (bf16[1,512,1024]{2,1,0:T(8,128)(2,1)S(1)}, bf16[1,512,1024]{2,1,0:T(8,128)(2,1)}, u32[]{:S(2)}) copy-start(bf16[1,512,1024]{2,1,0:T(8,128)(2,1)} %param.11) | copy-start | bytes 3145732
  41.8 111.0 %reduce-scatter.4.cloned.1.call-start = ((), (), s32[]{:S(2)}) async-start(), calls=%async_computation.7 | async-start | bytes 4718592 | tf_op jit(solution)/shard_map/reduce_scatter | solution.py:47
  46.3 0.7 copy-start.6
  46.3 1.1 copy-start.5
  46.4 163.1 %reduce-scatter.8.cloned.1.call-start = ((), (), s32[]{:S(2)}) async-start(), calls=%async_computation.10 | async-start | bytes 4718592 | tf_op jit(solution)/shard_map/reduce_scatter | solution.py:65
  69.1 1.0 copy-start.1
  73.3 180.5 %all-gather.4.cloned.1.call-start = ((), (), s32[]{:S(2)}) async-start(), calls=%async_computation.9 | async-start | bytes 2359296 | tf_op jit(solution)/shard_map/all_gather | solution.py:51
  212.0 89.7 %all-gather.8.cloned.1.call-start = ((), (), s32[]{:S(2)}) async-start(), calls=%async_computation.12 | async-start | bytes 2359296 | tf_op jit(solution)/shard_map/all_gather | solution.py:73
  212.6 137.3 %all-gather.6.cloned.1.call-start = ((), (), s32[]{:S(2)}) async-start(), calls=%async_computation.11 | async-start | bytes 2359296 | tf_op jit(solution)/shard_map/all_gather | solution.py:72
  257.6 99.5 %all-to-all-start.1 = ((bf16[32,32,512]{2,1,0:T(8,128)(2,1)}), bf16[32,32,512]{2,1,0:T(8,128)(2,1)}, u32[]{:S(2)}, u32[]{:S(2)}) async-start(bf16[32,32,512]{2,1,0:T(8,128)(2,1)} %fusion.20), calls=%async_computation.3 | async-start | bytes 2097152 | tf_op jit(solution)/shard_map/all_to_all | solution.py:55
  301.7 4.6 %copy-start.2 = (bf16[32,32,512]{2,1,0:T(8,128)(2,1)S(1)}, bf16[32,32,512]{2,1,0:T(8,128)(2,1)}, u32[]{:S(2)}) copy-start(bf16[32,32,512]{2,1,0:T(8,128)(2,1)} %copy-done.1) | copy-start | bytes 3145732
  301.7 4.6 %copy-start.7 = (bf16[32,1,32,1024]{3,2,0,1:T(8,128)(2,1)S(1)}, bf16[32,1,32,1024]{3,2,0,1:T(8,128)(2,1)}, u32[]{:S(2)}) copy-start(bf16[32,1,32,1024]{3,2,0,1:T(8,128)(2,1)} %all-gather.4.cloned.1.call-done) | copy-start | bytes 6291460
  349.8 5.0 %copy-start.3 = (bf16[32,1,32,1024]{3,2,0,1:T(8,128)(2,1)S(1)}, bf16[32,1,32,1024]{3,2,0,1:T(8,128)(2,1)}, u32[]{:S(2)}) copy-start(bf16[32,1,32,1024]{3,2,0,1:T(8,128)(2,1)} %all-gather.8.cloned.1.call-done) | copy-start | bytes 6291460
  357.0 29.3 %all-to-all-start.3 = ((bf16[32,32,512]{2,1,0:T(8,128)(2,1)}), bf16[32,32,512]{2,1,0:T(8,128)(2,1)}, u32[]{:S(2)}, u32[]{:S(2)}) async-start(bf16[32,32,512]{2,1,0:T(8,128)(2,1)} %add_convert_fusion), calls=%async_computation.6 | async-start | bytes 2097152 | tf_op jit(solution)/shard_map/all_to_all | solution.py:79
Sparse Core Ops, SparseCore 0:
  42.0 54.3 reduce-scatter.5
  98.9 53.9 reduce-scatter.3
  155.4 53.9 reduce-scatter.7
  212.1 41.6 all-gather.3
  255.3 46.3 all-gather.7
  303.8 45.9 all-gather.5
where the time goes:
time: 396 us; the launch traced here: 395 us
  waiting for transfers between devices  262 us (66%)
  blocking collectives  46.1 us (12%)
  matrix products  39.7 us (10%)
  starting transfers between devices  24.7 us (6%)
  between operations  14.2 us (4%)
  other arithmetic  5.89 us (1%)
    reduce_scatter x1, waiting for transfers between devices, local(): lax.psum_scatter(d_hidden_part, 'pipe', scatter_dimension=3, tiled=True)  56.6 us
    reduce_scatter x1, waiting for transfers between devices, local(): lax.psum_scatter(gate_part, 'pipe', scatter_dimension=3, tiled=True)  56.5 us
    all_gather x1, waiting for transfers between devices, local(): lax.all_gather(d_gate_share, 'pipe', axis=3, tiled=True)  41.2 us
    all_gather x1, waiting for transfers between devices, local(): hidden = lax.all_gather(hidden_share, 'pipe', axis=3, tiled=True)  40.6 us
    all_gather x1, waiting for transfers between devices, local(): lax.all_gather(d_up_share, 'pipe', axis=3, tiled=True)  31.9 us
    all_to_all x1, blocking collectives, local(): lax.all_to_all(outbound, ('dp', 'expert'), split_axis=0, concat_axis=0, t...  25.4 us
    reduce_scatter x1, waiting for transfers between devices, local(): lax.psum_scatter(up_part, 'pipe', scatter_dimension=3, tiled=True)  23 us
    all_to_all x1, blocking collectives, local(): lax.all_to_all(scaled_out, ('dp', 'expert'), split_axis=0, concat_axis=0,...  20.7 us
  transfers between devices with their start and end apart: 8, of which 7 were waited for; matrix products, arithmetic and copies ran while one was open for 8% of the time, Pallas kernels for 0%

commit v1 on v0

--- a/solution.py
+++ b/solution.py
@@ -48,7 +48,24 @@
         lax.psum_scatter(up_part, "pipe", scatter_dimension=3, tiled=True),
     )
     hidden_share = (jax.nn.silu(gate_share) * up_share).astype(jnp.bfloat16)
-    hidden = lax.all_gather(hidden_share, "pipe", axis=3, tiled=True)
+    ways, here, step = (lax.axis_size("pipe"), lax.axis_index("pipe"), hidden_share.shape[3])
+    lengths = [n * ways if d == 3 else n for d, n in enumerate(hidden_share.shape)]
+    hidden = lax.dynamic_update_slice_in_dim(
+        jnp.zeros(lengths, hidden_share.dtype), hidden_share, here * step, axis=3
+    )
+    going_up = going_down = hidden_share
+    for far in range(1, ways // 2 + 1):
+        going_up = lax.ppermute(going_up, "pipe", [(d, (d + 1) % ways) for d in range(ways)])
+        hidden = lax.dynamic_update_slice_in_dim(
+            hidden, going_up, (here - far) % ways * step, axis=3
+        )
+        if 2 * far < ways:
+            going_down = lax.ppermute(
+                going_down, "pipe", [(d, (d - 1) % ways) for d in range(ways)]
+            )
+            hidden = lax.dynamic_update_slice_in_dim(
+                hidden, going_down, (here + far) % ways * step, axis=3
+            )
     expert_out = jnp.einsum(
         "sjcf,jfd->sjcd", hidden, w_down, preferred_element_type=jnp.float32
     ).astype(jnp.bfloat16)

time: 396 us -> 355 us (0.90)
  waiting for transfers between devices: 262 us -> 207 us
  starting transfers between devices: 24.7 us -> 32.9 us
  local copies, waits for them, and re-layouts: 3.19 us -> 8.06 us
    all_gather x1 -> x0, waiting for transfers between devices: 40.6 us -> none  [local(): hidden = lax.all_gather(hidden_share, 'pipe', axis=3, tiled=True)]
    reduce_scatter x1, waiting for transfers between devices: 56.5 us -> 23 us  [local(): lax.psum_scatter(gate_part, 'pipe', scatter_dimension=3, tiled=True)]
    reduce_scatter x1, waiting for transfers between devices: 23 us -> 56.5 us  [local(): lax.psum_scatter(up_part, 'pipe', scatter_dimension=3, tiled=True)]
    all_gather x1, waiting for transfers between devices: 31.9 us -> 0.01 us  [local(): lax.all_gather(d_up_share, 'pipe', axis=3, tiled=True)]
    ppermute x0 -> x7, waiting for transfers between devices: none -> 28.4 us  [the longest x4 28.3 us: local(): lax.ppermute(going_up, 'pipe', [(d, (d + 1) % ways) for d in range(ways)])]
    all_gather x1, waiting for transfers between devices: 41.2 us -> 18.5 us  [local(): lax.all_gather(d_gate_share, 'pipe', axis=3, tiled=True)]
    all_to_all x1, waiting for transfers between devices: 0.01 us -> 12.8 us  [local(): lax.all_to_all(expert_out.reshape(num_experts, CAP, slice_width), ('dp',...]
    ppermute x0 -> x7, starting transfers between devices: none -> 10.6 us  [the longest x3 8.21 us: local(): lax.ppermute(going_down, 'pipe', [(d, (d - 1) % ways) for d in range(ways)])]
  transfers between devices with their start and end apart: 8 -> 14, of which waited for: 7 -> 10; matrix products, arithmetic and copies ran while one was open for 8% -> 9% of each run, Pallas kernels for 0% -> 0%
where the time goes in v1:
time: 355 us; the launch traced here: 354 us
  waiting for transfers between devices  207 us (58%)
  blocking collectives  46.1 us (13%)
  matrix products  40.2 us (11%)
  starting transfers between devices  32.9 us (9%)
  between operations  14.1 us (4%)
  local copies, waits for them, and re-layouts  8.06 us (2%)
  other arithmetic  5.83 us (2%)
    reduce_scatter x1, waiting for transfers between devices, local(): lax.psum_scatter(d_hidden_part, 'pipe', scatter_dimension=3, tiled=True)  56.6 us
    reduce_scatter x1, waiting for transfers between devices, local(): lax.psum_scatter(up_part, 'pipe', scatter_dimension=3, tiled=True)  56.5 us
    ppermute x4, waiting for transfers between devices, local(): lax.ppermute(going_up, 'pipe', [(d, (d + 1) % ways) for d in range(ways)])  28.3 us
    all_to_all x1, blocking collectives, local(): lax.all_to_all(outbound, ('dp', 'expert'), split_axis=0, concat_axis=0, t...  25.4 us
    reduce_scatter x1, waiting for transfers between devices, local(): lax.psum_scatter(gate_part, 'pipe', scatter_dimension=3, tiled=True)  23 us
    all_to_all x1, blocking collectives, local(): lax.all_to_all(scaled_out, ('dp', 'expert'), split_axis=0, concat_axis=0,...  20.7 us
    all_gather x1, waiting for transfers between devices, local(): lax.all_gather(d_gate_share, 'pipe', axis=3, tiled=True)  18.5 us
    all_to_all x1, waiting for transfers between devices, local(): lax.all_to_all(expert_out.reshape(num_experts, CAP, slice_width), ('dp',...  12.8 us
  transfers between devices with their start and end apart: 14, of which 10 were waited for; matrix products, arithmetic and copies ran while one was open for 9% of the time, Pallas kernels for 0%

profile of v1, /device:TPU:1, one launch (start us, length us, event | category | flops | bytes accessed | tf_op | source)
XLA Modules:
  0.0 353.9 jit_solution(17701921874020563196)
XLA Ops:
  7.2 0.0 reduce-scatter.4.cloned.1.call-start
  7.2 0.9 copy.64
  8.1 0.1 eq.52
  8.2 0.1 eq.48
  8.4 1.7 reduce-window.6
  10.1 0.3 slice_reduce_fusion
  10.4 0.1 fusion.37
  10.5 0.1 reduce_sum.30
  10.7 0.1 copy.67
  10.7 0.7 multiply_add_fusion
  11.5 0.4 convert_reduce_fusion
  11.8 1.3 convolution_convert_fusion
  13.2 25.4 %all_to_all.20 = bf16[32,32,512]{2,1,0:T(8,128)(2,1)S(1)} all-to-all(bf16[32,32,512]{2,1,0:T(8,128)(2,1)S(1)} %bitcast.118), channel_id=1, replica_groups=mesh['pipe'=8,'dp'=4,'expert'=8] {'dp','expert'}, dimensions={0} | all-to-all | bytes 2097152 | tf_op jit(solution)/shard_map/all_to_all | solution.py:37
  38.6 3.2 convolution_bitcast_fusion.2
  41.8 0.0 reduce-scatter.6.cloned.1.call-start
  41.9 4.5 %convolution_bitcast_fusion.1 = f32[32,1,32,1024]{3,2,0,1:T(8,128)} fusion(bf16[32,32,512]{2,1,0:T(8,128)(2,1)S(1)} %all_to_all.20, bf16[1,512,1024]{2,1,0:T(8,128)(2,1)} %param.11), kind=kOutput, calls=%fused_computation.4 | convolution fusion | flops 1073741824 | bytes 6291456 | tf_op jit(solution)/shard_map/sjcd,jdf->sjcf/dot_general | solution.py:45
  46.4 0.0 reduce-scatter.6.cloned.1.call-update
  46.4 0.0 reduce-scatter.8.cloned.1.call-start
  46.4 0.6 copy-done.6
  47.0 0.4 select_reduce_fusion
  47.4 1.0 convolution_convert_fusion.1
  48.4 20.7 %all_to_all.21 = bf16[32,32,512]{2,1,0:T(8,128)(2,1)S(1)} all-to-all(bf16[32,32,512]{2,1,0:T(8,128)(2,1)S(1)} %bitcast.119), channel_id=1, replica_groups=mesh['pipe'=8,'dp'=4,'expert'=8] {'dp','expert'}, dimensions={0} | all-to-all | bytes 2097152 | tf_op jit(solution)/shard_map/all_to_all | solution.py:38
  69.1 1.0 copy-done.1
  70.0 3.3 convolution_bitcast_fusion
  73.3 0.0 all-gather.5.cloned.1.call-start
  73.4 23.0 %reduce-scatter.4.cloned.1.call-done = f32[32,1,32,128]{3,2,0,1:T(8,128)} async-done(((f32[32,1,32,1024]{3,2,0,1:T(8,128)}), f32[32,1,32,128]{3,2,0,1:T(8,128)}) %reduce-scatter.4.cloned.1.call-update) | async-done | bytes 524304 | tf_op jit(solution)/shard_map/reduce_scatter | solution.py:47
  96.3 56.5 %reduce-scatter.6.cloned.1.call-done = f32[32,1,32,128]{3,2,0,1:T(8,128)} async-done(((f32[32,1,32,1024]{3,2,0,1:T(8,128)}), f32[32,1,32,128]{3,2,0,1:T(8,128)}) %reduce-scatter.6.cloned.1.call-update) | async-done | bytes 524304 | tf_op jit(solution)/shard_map/reduce_scatter | solution.py:48
  152.9 56.6 %reduce-scatter.8.cloned.1.call-done = f32[32,1,32,128]{3,2,0,1:T(8,128)} async-done(((f32[32,1,32,1024]{3,2,0,1:T(8,128)}), f32[32,1,32,128]{3,2,0,1:T(8,128)}) %reduce-scatter.8.cloned.1.call-update) | async-done | bytes 524304 | tf_op jit(solution)/shard_map/reduce_scatter | solution.py:82
  209.4 2.5 multiply_convert_fusion.1
  211.9 0.0 all-gather.5.cloned.1.call-update
  211.9 0.0 all-gather.3.cloned.1.call-start
  211.9 0.1 collective-permute-start
  212.2 2.5 collective-permute-start.1
  214.7 0.3 broadcast.40
  215.0 0.2 copy_dynamic-update-slice_fusion.7
  215.2 5.3 %collective-permute-done = bf16[32,1,32,128]{3,2,0,1:T(8,128)(2,1)} collective-permute-done((bf16[32,1,32,128]{3,2,0,1:T(8,128)(2,1)S(1)}, bf16[32,1,32,128]{3,2,0,1:T(8,128)(2,1)}, u32[]{:S(2)}, u32[]{:S(2)}) %collective-permute-start) | collective-permute-done | bytes 262176 | tf_op jit(solution)/shard_map/ppermute | solution.py:58
  220.5 1.1 copy_dynamic-update-slice_fusion.6
  221.6 2.8 collective-permute-start.3
  224.4 1.2 copy_dynamic-update-slice_fusion.5
  225.6 6.1 %collective-permute-done.2 = bf16[32,1,32,128]{3,2,0,1:T(8,128)(2,1)S(1)} collective-permute-done((bf16[32,1,32,128]{3,2,0,1:T(8,128)(2,1)}, bf16[32,1,32,128]{3,2,0,1:T(8,128)(2,1)S(1)}, u32[]{:S(2)}, u32[]{:S(2)}) %collective-permute-start.2) | collective-permute-done | bytes 262176 | tf_op jit(solution)/shard_map/ppermute | solution.py:58
  231.6 0.2 copy_dynamic-update-slice_fusion.4
  231.8 0.0 collective-permute-done.3
  231.8 2.9 collective-permute-start.5
  234.7 0.2 copy_dynamic-update-slice_fusion.3
  234.9 7.0 %collective-permute-done.4 = bf16[32,1,32,128]{3,2,0,1:T(8,128)(2,1)S(1)} collective-permute-done((bf16[32,1,32,128]{3,2,0,1:T(8,128)(2,1)S(1)}, bf16[32,1,32,128]{3,2,0,1:T(8,128)(2,1)S(1)}, u32[]{:S(2)}, u32[]{:S(2)}) %collective-permute-start.4) | collective-permute-done | bytes 262176 | tf_op jit(solution)/shard_map/ppermute | solution.py:58
  241.9 2.3 collective-permute-start.6
  244.3 0.2 copy_dynamic-update-slice_fusion.2
  244.4 0.2 copy_dynamic-update-slice_fusion.1
  244.6 9.9 %collective-permute-done.6 = bf16[32,1,32,128]{3,2,0,1:T(8,128)(2,1)S(1)} collective-permute-done((bf16[32,1,32,128]{3,2,0,1:T(8,128)(2,1)S(1)}, bf16[32,1,32,128]{3,2,0,1:T(8,128)(2,1)S(1)}, u32[]{:S(2)}, u32[]{:S(2)}) %collective-permute-start.6) | collective-permute-done | bytes 262176 | tf_op jit(solution)/shard_map/ppermute | solution.py:58
  254.5 0.2 copy_dynamic-update-slice_fusion
  254.7 1.3 copy-done.2
  256.1 2.4 fusion.16
  258.4 9.9 %all-to-all-start.1 = ((bf16[32,32,512]{2,1,0:T(8,128)(2,1)}), bf16[32,32,512]{2,1,0:T(8,128)(2,1)}, u32[]{:S(2)}, u32[]{:S(2)}) async-start(bf16[32,32,512]{2,1,0:T(8,128)(2,1)} %fusion.16), calls=%async_computation.3 | async-start | bytes 2097152 | tf_op jit(solution)/shard_map/all_to_all | solution.py:72
  268.4 4.3 %fusion.25 = bf16[1,1024,512]{2,1,0:T(8,128)(2,1)} fusion(bf16[32,32,1024]{2,0,1:T(8,128)(2,1)} %copy-done.2, bf16[32,32,512]{2,1,0:T(8,128)(2,1)} %copy-done.1), kind=kOutput, calls=%fused_computation.25 | convolution fusion | flops 1074266112 | bytes 4194304 | tf_op jit(solution)/shard_map/sjcf,sjcd->jfd/dot_general | solution.py:114
  272.6 12.8 %all-to-all-done.1 = bf16[32,32,512]{2,1,0:T(8,128)(2,1)} async-done(((bf16[32,32,512]{2,1,0:T(8,128)(2,1)}), bf16[32,32,512]{2,1,0:T(8,128)(2,1)}, u32[]{:S(2)}, u32[]{:S(2)}) %all-to-all-start.1) | async-done | bytes 1048608 | tf_op jit(solution)/shard_map/all_to_all | solution.py:72
  285.5 2.6 convolution_convert_fusion.3
  288.0 4.5 %fusion.2 = f32[32,32,512]{2,1,0:T(8,128)} fusion(bf16[32,1,32,1024]{3,2,0,1:T(8,128)(2,1)} %all-gather.5.cloned.1.call-done, bf16[1,512,1024]{2,1,0:T(8,128)(2,1)} %param.11), kind=kOutput, calls=%fused_computation.11 | convolution fusion | flops 1073741824 | bytes 5242880 | tf_op jit(solution)/shard_map/sjcf,jdf->sjcd/dot_general | solution.py:94
  292.5 18.5 %all-gather.3.cloned.1.call-done = bf16[32,1,32,1024]{3,2,0,1:T(8,128)(2,1)} async-done(((bf16[32,1,32,128]{3,2,0,1:T(8,128)(2,1)}), bf16[32,1,32,1024]{3,2,0,1:T(8,128)(2,1)}) %all-gather.3.cloned.1.call-update) | async-done | bytes 2097168 | tf_op jit(solution)/shard_map/all_gather | solution.py:89
  311.0 4.8 %add_convert_fusion = bf16[32,32,512]{2,1,0:T(8,128)(2,1)} fusion(f32[32,32,512]{2,1,0:T(8,128)} %fusion.2, bf16[32,1,32,1024]{3,2,0,1:T(8,128)(2,1)} %all-gather.3.cloned.1.call-done, bf16[1,512,1024]{2,1,0:T(8,128)(2,1)} %param.10), kind=kOutput, calls=%fused_computation.19 | convolution fusion | flops 1074790400 | bytes 6291456 | tf_op jit(solution)/shard_map/sjcf,jdf->sjcd/dot_general | solution.py:93
  315.8 12.2 %all-to-all-start.3 = ((bf16[32,32,512]{2,1,0:T(8,128)(2,1)}), bf16[32,32,512]{2,1,0:T(8,128)(2,1)}, u32[]{:S(2)}, u32[]{:S(2)}) async-start(bf16[32,32,512]{2,1,0:T(8,128)(2,1)} %add_convert_fusion), calls=%async_computation.6 | async-start | bytes 2097152 | tf_op jit(solution)/shard_map/all_to_all | solution.py:96
  328.0 4.0 %fusion.19 = bf16[1,512,1024]{2,1,0:T(8,128)(2,1)} fusion(bf16[32,32,512]{2,1,0:T(8,128)(2,1)S(1)} %all_to_all.20, bf16[32,1,32,1024]{3,2,0,1:T(8,128)(2,1)} %all-gather.3.cloned.1.call-done), kind=kOutput, calls=%fused_computation.23 | convolution fusion | flops 1074266112 | bytes 4194304 | tf_op jit(solution)/shard_map/sjcd,sjcf->jdf/dot_general | solution.py:108
  332.0 2.3 fusion.22
  334.3 10.8 %all-to-all-done.3 = bf16[32,32,512]{2,1,0:T(8,128)(2,1)} async-done(((bf16[32,32,512]{2,1,0:T(8,128)(2,1)}), bf16[32,32,512]{2,1,0:T(8,128)(2,1)}, u32[]{:S(2)}, u32[]{:S(2)}) %all-to-all-start.3) | async-done | bytes 1048608 | tf_op jit(solution)/shard_map/all_to_all | solution.py:96
  345.1 2.2 convolution_convert_fusion.2
  (21 shorter events, 0.1 us)
Async XLA Ops:
  7.2 62.9 %copy-start = (bf16[1,1024,512]{2,1,0:T(8,128)(2,1)S(1)}, bf16[1,1024,512]{2,1,0:T(8,128)(2,1)}, u32[]{:S(2)}) copy-start(bf16[1,1024,512]{2,1,0:T(8,128)(2,1)} %param.12) | copy-start | bytes 3145732
  7.2 89.1 %reduce-scatter.4.cloned.1.call-start = ((), (), s32[]{:S(2)}) async-start(), calls=%async_computation.7 | async-start | bytes 4718592 | tf_op jit(solution)/shard_map/reduce_scatter | solution.py:47
  11.5 27.1 %copy-start.4 = (bf16[1,512,1024]{2,1,0:T(8,128)(2,1)S(1)}, bf16[1,512,1024]{2,1,0:T(8,128)(2,1)}, u32[]{:S(2)}) copy-start(bf16[1,512,1024]{2,1,0:T(8,128)(2,1)} %param.10) | copy-start | bytes 3145732
  41.8 111.0 %reduce-scatter.6.cloned.1.call-start = ((), (), s32[]{:S(2)}) async-start(), calls=%async_computation.8 | async-start | bytes 4718592 | tf_op jit(solution)/shard_map/reduce_scatter | solution.py:48
  46.4 0.7 copy-start.6
  46.4 1.1 copy-start.5
  46.4 163.0 %reduce-scatter.8.cloned.1.call-start = ((), (), s32[]{:S(2)}) async-start(), calls=%async_computation.9 | async-start | bytes 4718592 | tf_op jit(solution)/shard_map/reduce_scatter | solution.py:82
  69.1 1.0 copy-start.1
  73.3 214.7 %all-gather.5.cloned.1.call-start = ((), (), s32[]{:S(2)}) async-start(), calls=%async_computation.11 | async-start | bytes 2359296 | tf_op jit(solution)/shard_map/all_gather | solution.py:90
  211.9 99.1 %all-gather.3.cloned.1.call-start = ((), (), s32[]{:S(2)}) async-start(), calls=%async_computation.10 | async-start | bytes 2359296 | tf_op jit(solution)/shard_map/all_gather | solution.py:89
  211.9 8.5 %collective-permute-start = (bf16[32,1,32,128]{3,2,0,1:T(8,128)(2,1)S(1)}, bf16[32,1,32,128]{3,2,0,1:T(8,128)(2,1)}, u32[]{:S(2)}, u32[]{:S(2)}) collective-permute-start(bf16[32,1,32,128]{3,2,0,1:T(8,128)(2,1)S(1)} %get-tuple-element.6), channel_id=1, source_target_pairs={{0,32},{32,64},{64,96},{96,128},{128,160},{160,192},{192,224},{224... | collective-permute-start | bytes 786440 | tf_op jit(solution)/shard_map/ppermute | solution.py:58
  212.2 9.5 %collective-permute-start.1 = (bf16[32,1,32,128]{3,2,0,1:T(8,128)(2,1)S(1)}, bf16[32,1,32,128]{3,2,0,1:T(8,128)(2,1)}, u32[]{:S(2)}, u32[]{:S(2)}) collective-permute-start(bf16[32,1,32,128]{3,2,0,1:T(8,128)(2,1)S(1)} %get-tuple-element.6), channel_id=1, source_target_pairs={{0,224},{32,0},{64,32},{96,64},{128,96},{160,128},{192,160},{224,1... | collective-permute-start | bytes 786440 | tf_op jit(solution)/shard_map/ppermute | solution.py:63
  220.5 11.1 %collective-permute-start.2 = (bf16[32,1,32,128]{3,2,0,1:T(8,128)(2,1)}, bf16[32,1,32,128]{3,2,0,1:T(8,128)(2,1)S(1)}, u32[]{:S(2)}, u32[]{:S(2)}) collective-permute-start(bf16[32,1,32,128]{3,2,0,1:T(8,128)(2,1)} %collective-permute-done), channel_id=1, source_target_pairs={{0,32},{32,64},{64,96},{96,128},{128,160},{160,192},{192,224},{224... | collective-permute-start | bytes 786440 | tf_op jit(solution)/shard_map/ppermute | solution.py:58
  221.6 10.2 %collective-permute-start.3 = (bf16[32,1,32,128]{3,2,0,1:T(8,128)(2,1)}, bf16[32,1,32,128]{3,2,0,1:T(8,128)(2,1)S(1)}, u32[]{:S(2)}, u32[]{:S(2)}) collective-permute-start(bf16[32,1,32,128]{3,2,0,1:T(8,128)(2,1)} %collective-permute-done.1), channel_id=1, source_target_pairs={{0,224},{32,0},{64,32},{96,64},{128,96},{160,128},{192,160},{224,1... | collective-permute-start | bytes 786440 | tf_op jit(solution)/shard_map/ppermute | solution.py:63
  231.6 10.3 %collective-permute-start.4 = (bf16[32,1,32,128]{3,2,0,1:T(8,128)(2,1)S(1)}, bf16[32,1,32,128]{3,2,0,1:T(8,128)(2,1)S(1)}, u32[]{:S(2)}, u32[]{:S(2)}) collective-permute-start(bf16[32,1,32,128]{3,2,0,1:T(8,128)(2,1)S(1)} %collective-permute-done.2), channel_id=1, source_target_pairs={{0,32},{32,64},{64,96},{96,128},{128,160},{160,192},{192,224},{224... | collective-permute-start | bytes 786440 | tf_op jit(solution)/shard_map/ppermute | solution.py:58
  231.8 12.6 %collective-permute-start.5 = (bf16[32,1,32,128]{3,2,0,1:T(8,128)(2,1)S(1)}, bf16[32,1,32,128]{3,2,0,1:T(8,128)(2,1)S(1)}, u32[]{:S(2)}, u32[]{:S(2)}) collective-permute-start(bf16[32,1,32,128]{3,2,0,1:T(8,128)(2,1)S(1)} %collective-permute-done.3), channel_id=1, source_target_pairs={{0,224},{32,0},{64,32},{96,64},{128,96},{160,128},{192,160},{224,1... | collective-permute-start | bytes 786440 | tf_op jit(solution)/shard_map/ppermute | solution.py:63
  241.9 12.6 %collective-permute-start.6 = (bf16[32,1,32,128]{3,2,0,1:T(8,128)(2,1)S(1)}, bf16[32,1,32,128]{3,2,0,1:T(8,128)(2,1)S(1)}, u32[]{:S(2)}, u32[]{:S(2)}) collective-permute-start(bf16[32,1,32,128]{3,2,0,1:T(8,128)(2,1)S(1)} %collective-permute-done.4), channel_id=1, source_target_pairs={{0,32},{32,64},{64,96},{96,128},{128,160},{160,192},{192,224},{224... | collective-permute-start | bytes 786440 | tf_op jit(solution)/shard_map/ppermute | solution.py:58
  254.7 1.3 copy-start.2
  258.4 27.1 %all-to-all-start.1 = ((bf16[32,32,512]{2,1,0:T(8,128)(2,1)}), bf16[32,32,512]{2,1,0:T(8,128)(2,1)}, u32[]{:S(2)}, u32[]{:S(2)}) async-start(bf16[32,32,512]{2,1,0:T(8,128)(2,1)} %fusion.16), calls=%async_computation.3 | async-start | bytes 2097152 | tf_op jit(solution)/shard_map/all_to_all | solution.py:72
  315.8 29.3 %all-to-all-start.3 = ((bf16[32,32,512]{2,1,0:T(8,128)(2,1)}), bf16[32,32,512]{2,1,0:T(8,128)(2,1)}, u32[]{:S(2)}, u32[]{:S(2)}) async-start(bf16[32,32,512]{2,1,0:T(8,128)(2,1)} %add_convert_fusion), calls=%async_computation.6 | async-start | bytes 2097152 | tf_op jit(solution)/shard_map/all_to_all | solution.py:96
  328.0 4.0 %copy-start.3 = (bf16[32,1,32,1024]{3,2,0,1:T(8,128)(2,1)S(1)}, bf16[32,1,32,1024]{3,2,0,1:T(8,128)(2,1)}, u32[]{:S(2)}) copy-start(bf16[32,1,32,1024]{3,2,0,1:T(8,128)(2,1)} %all-gather.5.cloned.1.call-done) | copy-start | bytes 6291460
Sparse Core Ops, SparseCore 0:
  42.0 54.3 reduce-scatter.3
  98.9 53.9 reduce-scatter.5
  155.4 53.9 reduce-scatter.7
  212.0 51.5 all-gather.4
  265.2 45.7 all-gather.2
